TPU v7x, 128 devices: a whole 4x4x4 slice. The times are simulated.
128 devices in a mesh: replica: 4 (over z), shard: 16 (over y, x_lo, core), tensor: 2 (over x_hi).
Axes of the slice: x: 4 (x_hi: 2, x_lo: 2; x = x_hi * 2 + x_lo), y: 4, z: 4, core: 2. Of those that a mesh axis runs over, the one named last changes fastest.
Arguments:
- trained_up: bfloat16 [4, 1024, 4096], P('replica', None, 'tensor'), may hold values from -6 to 6
- trained_down: bfloat16 [4, 4096, 1024], P('replica', 'tensor'), may hold values from -6 to 6
- trained_embed: bfloat16 [4, 32768, 1024], P('replica', ('shard', 'tensor')), may hold values from -6 to 6
- trained_norm: bfloat16 [4, 2, 1024], P('replica'), may hold values from 0.099609375 to 1.8984375
- master_up: float32 [1024, 4096], P(('replica', 'shard', 'tensor')), may hold values from -6 to 6
- moment_up: float32 [1024, 4096], P(('replica', 'shard', 'tensor')), may hold values from -4 to 4
- master_down: float32 [2, 2048, 1024], P('tensor', ('replica', 'shard')), may hold values from -6 to 6
- moment_down: float32 [2, 2048, 1024], P('tensor', ('replica', 'shard')), may hold values from -4 to 4
- master_embed: float32 [32, 1024, 1024], P(('shard', 'tensor'), 'replica'), may hold values from -6 to 6
- moment_embed: float32 [32, 1024, 64], P(('shard', 'tensor'), 'replica'), may hold values from -4 to 4
- master_norm: float32 [2, 1024], replicated, may hold values from 0.1 to 1.9
- moment_norm: float32 [2, 1024], replicated, may hold values from -2 to 2
- embed_basis: float32 [1024, 64], replicated, may hold values from -0.1875 to 0.1875
Outputs:
- recast_up: bfloat16 [1024, 4096], P(None, 'tensor')
- recast_down: bfloat16 [4096, 1024], P('tensor')
- recast_embed: bfloat16 [32768, 1024], P(('shard', 'tensor'))
- recast_norm: bfloat16 [2, 1024], replicated
- stored_up: float32 [1024, 4096], P(('replica', 'shard', 'tensor'))
- velocity_up: float32 [1024, 4096], P(('replica', 'shard', 'tensor'))
- stored_down: float32 [2, 2048, 1024], P('tensor', ('replica', 'shard'))
- velocity_down: float32 [2, 2048, 1024], P('tensor', ('replica', 'shard'))
- stored_embed: float32 [32, 1024, 1024], P(('shard', 'tensor'), 'replica')
- velocity_embed: float32 [32, 1024, 64], P(('shard', 'tensor'), 'replica')
- stored_norm: float32 [2, 1024], replicated
- velocity_norm: float32 [2, 1024], replicated
All inputs are finite; a program needn't handle non-finite values.
Results may differ from a plain program's by a relative error of at most 0.012.
Values may be sent and summed in bfloat16 or wider, within the bound.
A program may use at most 128 MiB of HBM per device.

v0:
```python
import jax
import jax.numpy as jnp
from jax import lax
from jax.sharding import PartitionSpec as P


def outer_step(master, moment, summed, groups):
    difference = master - summed / groups
    velocity = 0.5 * moment + difference
    return (master - 0.7 * (difference + 0.5 * velocity), velocity)


def body(
    trained_up,
    trained_down,
    trained_embed,
    trained_norm,
    master_up,
    moment_up,
    master_down,
    moment_down,
    master_embed,
    moment_embed,
    master_norm,
    moment_norm,
    embed_basis,
):
    replicas = lax.axis_size("replica")
    shards = lax.axis_size("shard")
    tensors = lax.axis_size("tensor")
    shard_pos = lax.axis_index("shard")
    width = embed_basis.shape[0]
    rows_up = master_up.shape[0]
    half_cols = trained_up.shape[2]
    rows_down = master_down.shape[1]
    up_blocks = trained_up[0].reshape(replicas, shards, tensors, rows_up, half_cols)
    up_own = lax.dynamic_index_in_dim(up_blocks, shard_pos, 1, keepdims=False)
    down_blocks = trained_down[0].reshape(replicas, shards, rows_down, width)
    down_own = lax.dynamic_index_in_dim(down_blocks, shard_pos, 1, keepdims=False)
    up_summed, down_summed = (
        lax.psum_scatter(
            up_own.astype(jnp.float32).astype(jnp.bfloat16),
            "replica",
            scatter_dimension=0,
            tiled=True,
        ).astype(jnp.float32),
        lax.psum_scatter(
            down_own.astype(jnp.float32).astype(jnp.bfloat16),
            "replica",
            scatter_dimension=0,
            tiled=True,
        ).astype(jnp.float32),
    )
    up_summed = lax.all_to_all(up_summed, "tensor", split_axis=1, concat_axis=3, tiled=True)
    stored_up, velocity_up = outer_step(
        master_up, moment_up, up_summed.reshape(rows_up, half_cols * tensors), replicas
    )
    stored_down, velocity_down = outer_step(master_down, moment_down, down_summed, replicas)
    norm_summed = lax.psum(trained_norm[0].astype(jnp.float32), "replica")
    stored_norm, velocity_norm = outer_step(master_norm, moment_norm, norm_summed, replicas)
    embed_own = master_embed[0]
    rows_embed = embed_own.shape[0]
    embed_terms = trained_embed[0].reshape(replicas, rows_embed, width).astype(jnp.float32)
    embed_summed = lax.psum_scatter(
        embed_terms.astype(jnp.bfloat16), "replica", scatter_dimension=0, tiled=True
    ).astype(jnp.float32)[0]
    coefficient = jnp.dot(
        embed_own - embed_summed / replicas, embed_basis, precision=lax.Precision.HIGHEST
    )
    velocity_rows = 0.5 * moment_embed[0] + coefficient
    stored_rows = embed_own - 0.7 * jnp.dot(
        coefficient + 0.5 * velocity_rows, embed_basis.T, precision=lax.Precision.HIGHEST
    )
    up_piece = lax.all_to_all(
        stored_up.astype(jnp.bfloat16), "tensor", split_axis=1, concat_axis=0, tiled=True
    )
    down_piece = stored_down[0].astype(jnp.bfloat16)
    recast_up, recast_down = (
        lax.all_gather(up_piece, ("replica", "shard"), axis=0, tiled=True),
        lax.all_gather(down_piece, ("replica", "shard"), axis=0, tiled=True),
    )
    recast_embed = lax.all_gather(stored_rows.astype(jnp.bfloat16), "replica", axis=0, tiled=True)
    return (
        recast_up,
        recast_down,
        recast_embed,
        stored_norm.astype(jnp.bfloat16),
        stored_up,
        velocity_up,
        stored_down,
        velocity_down,
        stored_rows[None],
        velocity_rows[None],
        stored_norm,
        velocity_norm,
    )


def solution(mesh):
    in_specs = (
        P("replica", None, "tensor"),
        P("replica", "tensor", None),
        P("replica", ("shard", "tensor"), None),
        P("replica", None, None),
        P(("replica", "shard", "tensor"), None),
        P(("replica", "shard", "tensor"), None),
        P("tensor", ("replica", "shard"), None),
        P("tensor", ("replica", "shard"), None),
        P(("shard", "tensor"), "replica", None),
        P(("shard", "tensor"), "replica", None),
        P(),
        P(),
        P(),
    )
    out_specs = (
        P(None, "tensor"),
        P("tensor", None),
        P(("shard", "tensor"), None),
        P(),
        P(("replica", "shard", "tensor"), None),
        P(("replica", "shard", "tensor"), None),
        P("tensor", ("replica", "shard"), None),
        P("tensor", ("replica", "shard"), None),
        P(("shard", "tensor"), "replica", None),
        P(("shard", "tensor"), "replica", None),
        P(),
        P(),
    )
    return jax.shard_map(body, mesh=mesh, in_specs=in_specs, out_specs=out_specs, check_vma=False)
```

profile of v0, /device:TPU:1, one launch (start us, length us, event | category | flops | bytes accessed | tf_op | source)
XLA Modules:
  0.0 376.6 jit_solution(8853071086595991756)
XLA Ops:
  7.2 0.0 copy-start
  7.2 0.0 copy-start.1
  7.2 0.0 copy-start.4
  7.2 0.0 reduce-scatter.6.cloned.1.call-start
  7.3 0.0 copy-start.12
  7.3 0.7 reduce-scatter.6.cloned.1.call-update
  7.9 0.0 copy-start.7
  8.0 0.0 copy-start.8
  8.0 0.0 all-reduce.3.cloned.1.call-start
  8.0 1.7 copy_bitcast_fusion
  9.7 0.0 copy-start.5
  9.7 0.0 copy-start.6
  9.7 0.0 all-reduce.3.cloned.1.call-update
  9.7 0.0 reduce-scatter.4.cloned.1.call-start
  9.8 0.0 copy-start.11
  9.8 1.7 dynamic-slice_bitcast_fusion
  11.5 0.0 copy-start.9
  11.5 0.0 copy-start.10
  11.5 0.0 reduce-scatter.4.cloned.1.call-update
  11.5 0.0 all-gather.7.cloned.1.call-start
  11.6 32.1 %reduce-scatter.6.cloned.1.call-done = bf16[1,256,1024]{2,1,0:T(8,128)(2,1)} async-done(((bf16[4,256,1024]{2,1,0:T(8,128)(2,1)}), bf16[1,256,1024]{2,1,0:T(8,128)(2,1)}) %reduce-scatter.6.cloned.1.call-update) | async-done | bytes 524304 | tf_op jit(solution)/shard_map/reduce_scatter | solution.py:64
  43.6 0.0 copy-done
  43.6 0.0 copy-done.1
  43.6 2.2 fusion.1
  45.8 0.0 copy-done.4
  45.8 2.2 fusion.16
  48.0 0.0 all-gather.7.cloned.1.call-update
  48.1 0.0 all-gather.5.cloned.1.call-start
  48.1 0.0 copy-done.12
  48.1 0.6 dynamic-slice
  48.7 37.3 %all-reduce.3.cloned.1.call-done = bf16[4,2,8,2048]{3,2,0,1:T(8,128)(2,1)} async-done(((bf16[4,2,8,2048]{3,2,0,1:T(8,128)(2,1)}), bf16[4,2,8,2048]{3,2,0,1:T(8,128)(2,1)}) %all-reduce.3.cloned.1.call-update) | async-done | bytes 262160
  86.0 1.5 dynamic-slice_convert_fusion
  87.5 8.6 %all_to_all.28 = f32[1,2,8,2048]{3,2,0,1:T(8,128)S(1)} all-to-all(f32[1,2,8,2048]{3,2,0,1:T(8,128)S(1)} %dynamic-slice_convert_fusion), channel_id=1, replica_groups=mesh['replica'=4,'shard'=16,'tensor'=2] {'tensor'}, dimensions={1} | all-to-all | bytes 262144 | tf_op jit(solution)/shard_map/all_to_all | solution.py:54
  96.1 0.0 copy-done.7
  96.1 0.0 copy-done.8
  96.1 0.7 fusion.15
  96.9 7.5 %all_to_all.29 = bf16[8,2,2048]{2,0,1:T(8,128)(2,1)} all-to-all(bf16[8,2,2048]{2,0,1:T(8,128)(2,1)S(1)} %bitcast.53), channel_id=1, replica_groups=mesh['replica'=4,'shard'=16,'tensor'=2] {'tensor'}, dimensions={1} | all-to-all | bytes 131072 | tf_op jit(solution)/shard_map/all_to_all | solution.py:74
  104.4 0.0 all-gather.5.cloned.1.call-update
  104.4 0.0 all-gather.9.cloned.1.call-start
  104.4 5.8 %reduce-scatter.4.cloned.1.call-done = bf16[1,32,1024]{2,1,0:T(8,128)(2,1)} async-done(((bf16[4,32,1024]{2,1,0:T(8,128)(2,1)}), bf16[1,32,1024]{2,1,0:T(8,128)(2,1)}) %reduce-scatter.4.cloned.1.call-update) | async-done | bytes 65552 | tf_op jit(solution)/shard_map/reduce_scatter | solution.py:47
  110.3 0.0 copy-done.5
  110.3 0.0 copy-done.6
  110.3 1.6 fusion.14
  111.9 0.0 all-gather.9.cloned.1.call-update
  111.9 0.0 copy-done.11
  111.9 6.9 %psum.7 = f32[2,1024]{1,0:T(2,128)S(1)} all-reduce(f32[2,1024]{1,0:T(2,128)S(1)} %bitcast_convert_fusion), channel_id=1, replica_groups=mesh['replica'=4,'shard'=16,'tensor'=2] {'replica'}, use_global_device_ids=true, to_apply=%region_3.4 | all-reduce | flops 2048 | bytes 16384 | tf_op jit(solution)/shard_map/psum | solution.py:59
  118.9 0.0 copy-done.9
  118.9 0.0 copy-done.10
  118.9 0.6 fusion.13
  119.5 0.6 fusion.8
  120.2 25.0 %all-gather.7.cloned.1.call-done = bf16[1024,1024]{1,0:T(8,128)(2,1)} async-done(((bf16[256,1024]{1,0:T(8,128)(2,1)}), bf16[1024,1024]{1,0:T(8,128)(2,1)}) %all-gather.7.cloned.1.call-update) | async-done | bytes 2097168 | tf_op jit(solution)/shard_map/all_gather | solution.py:82
  145.2 108.0 %all-gather.5.cloned.1.call-done = bf16[1024,2048]{1,0:T(8,128)(2,1)} async-done(((bf16[16,2048]{1,0:T(8,128)(2,1)}), bf16[1024,2048]{1,0:T(8,128)(2,1)}) %all-gather.5.cloned.1.call-update) | async-done | bytes 4194320 | tf_op jit(solution)/shard_map/all_gather | solution.py:79
  253.2 107.3 %all-gather.9.cloned.1.call-done = bf16[1,2048,1024]{2,1,0:T(8,128)(2,1)} async-done(((bf16[1,32,1024]{2,1,0:T(8,128)(2,1)}), bf16[1,2048,1024]{2,1,0:T(8,128)(2,1)}) %all-gather.9.cloned.1.call-update) | async-done | bytes 4194320 | tf_op jit(solution)/shard_map/all_gather | solution.py:80
  360.4 0.0 copy-start.2
  360.4 4.9 %copy.39 = bf16[1024,2048]{1,0:T(8,128)(2,1)} copy(bf16[1024,2048]{1,0:T(8,128)(2,1)} %all-gather.5.cloned.1.call-done) | data formatting | bytes 8388608
  365.4 0.0 copy-done.2
  365.4 0.0 copy-start.3
  365.4 2.1 copy.40
  367.5 1.0 copy-done.3
  368.5 1.3 copy.41
  (2 shorter events, 0.0 us)
Async XLA Ops:
  7.2 36.5 %copy-start = (f32[1024,64]{0,1:T(8,128)S(1)}, f32[1024,64]{0,1:T(8,128)}, u32[]{:S(2)}) copy-start(f32[1024,64]{0,1:T(8,128)} %param.25) | copy-start | bytes 786436
  7.2 36.5 %copy-start.1 = (f32[1,256,1024]{2,1,0:T(8,128)S(1)}, f32[1,256,1024]{2,1,0:T(8,128)}, u32[]{:S(2)}) copy-start(f32[1,256,1024]{2,1,0:T(8,128)} %param.21) | copy-start | bytes 3145732
  7.2 38.6 %copy-start.4 = (f32[1,256,64]{1,2,0:T(8,128)S(1)}, f32[1,256,64]{1,2,0:T(8,128)}, u32[]{:S(2)}) copy-start(f32[1,256,64]{1,2,0:T(8,128)} %param.22) | copy-start | bytes 196612
  7.2 36.4 %reduce-scatter.6.cloned.1.call-start = ((), (), s32[]{:S(2)}) async-start(), calls=%async_computation.6 | async-start | bytes 2621440 | tf_op jit(solution)/shard_map/reduce_scatter | solution.py:64
  7.3 40.9 %copy-start.12 = (u32[128]{0:T(128)S(1)}, u32[128]{0:T(128)}, u32[]{:S(2)}) copy-start(u32[128]{0:T(128)} %constant.47) | copy-start | bytes 1540
  7.9 88.2 %copy-start.7 = (f32[8,4096]{1,0:T(8,128)S(1)}, f32[8,4096]{1,0:T(8,128)}, u32[]{:S(2)}) copy-start(f32[8,4096]{1,0:T(8,128)} %param.17) | copy-start | bytes 393220
  8.0 88.2 %copy-start.8 = (f32[8,4096]{1,0:T(8,128)S(1)}, f32[8,4096]{1,0:T(8,128)}, u32[]{:S(2)}) copy-start(f32[8,4096]{1,0:T(8,128)} %param.18) | copy-start | bytes 393220
  8.0 78.0 %all-reduce.3.cloned.1.call-start = ((), (), s32[]{:S(2)}) async-start(), calls=%async_computation.9 | async-start | bytes 524288
  9.7 100.6 %copy-start.5 = (f32[1,32,1024]{2,1,0:T(8,128)S(1)}, f32[1,32,1024]{2,1,0:T(8,128)}, u32[]{:S(2)}) copy-start(f32[1,32,1024]{2,1,0:T(8,128)} %param.19) | copy-start | bytes 393220
  9.7 100.6 %copy-start.6 = (f32[1,32,1024]{2,1,0:T(8,128)S(1)}, f32[1,32,1024]{2,1,0:T(8,128)}, u32[]{:S(2)}) copy-start(f32[1,32,1024]{2,1,0:T(8,128)} %param.20) | copy-start | bytes 393220
  9.7 100.6 %reduce-scatter.4.cloned.1.call-start = ((), (), s32[]{:S(2)}) async-start(), calls=%async_computation.5 | async-start | bytes 327680 | tf_op jit(solution)/shard_map/reduce_scatter | solution.py:47
  9.8 102.1 %copy-start.11 = (bf16[1,2,1024]{2,1,0:T(2,128)(2,1)S(1)}, bf16[1,2,1024]{2,1,0:T(2,128)(2,1)}, u32[]{:S(2)}) copy-start(bf16[1,2,1024]{2,1,0:T(2,128)(2,1)} %param.16) | copy-start | bytes 12292
  11.5 107.4 %copy-start.9 = (f32[2,1024]{1,0:T(2,128)S(1)}, f32[2,1024]{1,0:T(2,128)}, u32[]{:S(2)}) copy-start(f32[2,1024]{1,0:T(2,128)} %param.23) | copy-start | bytes 24580
  11.5 107.4 %copy-start.10 = (f32[2,1024]{1,0:T(2,128)S(1)}, f32[2,1024]{1,0:T(2,128)}, u32[]{:S(2)}) copy-start(f32[2,1024]{1,0:T(2,128)} %param.24) | copy-start | bytes 24580
  11.5 133.6 %all-gather.7.cloned.1.call-start = ((), (), s32[]{:S(2)}) async-start(), calls=%async_computation.7 | async-start | bytes 2621440 | tf_op jit(solution)/shard_map/all_gather | solution.py:82
  48.1 205.1 %all-gather.5.cloned.1.call-start = ((), (), s32[]{:S(2)}) async-start(), calls=%async_computation.4 | async-start | bytes 4259840 | tf_op jit(solution)/shard_map/all_gather | solution.py:79
  104.4 256.0 %all-gather.9.cloned.1.call-start = ((), (), s32[]{:S(2)}) async-start(), calls=%async_computation.8 | async-start | bytes 4259840 | tf_op jit(solution)/shard_map/all_gather | solution.py:80
  360.4 4.9 %copy-start.2 = (bf16[1,2048,1024]{2,1,0:T(8,128)(2,1)S(1)}, bf16[1,2048,1024]{2,1,0:T(8,128)(2,1)}, u32[]{:S(2)}) copy-start(bf16[1,2048,1024]{2,1,0:T(8,128)(2,1)} %all-gather.9.cloned.1.call-done) | copy-start | bytes 12582916
  365.4 3.1 copy-start.3
Sparse Core Ops, SparseCore 0:
  10.4 33.1 reduce-scatter.5
  46.7 39.3 all-reduce.2
  89.0 21.2 reduce-scatter.3
  112.5 32.6 all-gather.6
  146.9 106.2 all-gather.4
  255.4 104.9 all-gather.8
where the time goes:
time: 377 us
  waiting for transfers between devices  316 us (84%)
  blocking collectives  23 us (6%)
  between operations  14.3 us (4%)
  local copies, waits for them, and re-layouts  13.4 us (4%)
  other arithmetic  5.09 us (1%)
  matrix products  4.38 us (1%)
    all_gather x1, waiting for transfers between devices, body(): lax.all_gather(up_piece, ('replica', 'shard'), axis=0, tiled=True)  108 us
    all_gather x1, waiting for transfers between devices, body(): lax.all_gather(down_piece, ('replica', 'shard'), axis=0, tiled=True)  107 us
    unnamed x7, waiting for transfers between devices  38.1 us
    reduce_scatter x1, waiting for transfers between devices, body(): lax.psum_scatter(embed_terms.astype(jnp.bfloat16), 'replica', scatter_dim...  32.1 us
    all_gather x1, waiting for transfers between devices, body(): lax.all_gather(stored_rows.astype(jnp.bfloat16), 'replica', axis=0, tiled...  25 us
    unnamed x30, local copies, waits for them, and re-layouts  10 us
    all_to_all x1, blocking collectives, body(): lax.all_to_all(up_summed, 'tensor', split_axis=1, concat_axis=3, tiled=True)  8.59 us
  transfers between devices with their start and end apart: 6, of which 6 were waited for; matrix products, arithmetic and copies ran while one was open for 4% of the time, Pallas kernels for 0%

commit v1 on v0

--- a/solution.py
+++ b/solution.py
@@ -77,7 +77,15 @@
     down_piece = stored_down[0].astype(jnp.bfloat16)
     recast_up, recast_down = (
         lax.all_gather(up_piece, ("replica", "shard"), axis=0, tiled=True),
-        lax.all_gather(down_piece, ("replica", "shard"), axis=0, tiled=True),
+        jnp.concatenate(
+            lax.all_to_all(
+                jnp.stack([down_piece for _ in range(lax.axis_size(("replica", "shard")))], axis=0),
+                split_axis=0,
+                concat_axis=0,
+                axis_name=("replica", "shard"),
+            ),
+            0,
+        ),
     )
     recast_embed = lax.all_gather(stored_rows.astype(jnp.bfloat16), "replica", axis=0, tiled=True)
     return (

time: 377 us -> 315 us (0.84)
  waiting for transfers between devices: 316 us -> 191 us
  blocking collectives: 23 us -> 72.7 us
  starting transfers between devices: 0.24 us -> 9.87 us
  local copies, waits for them, and re-layouts: 13.4 us -> 17.5 us
    all_gather x1 -> x0, waiting for transfers between devices: 107 us -> none  [body(): lax.all_gather(down_piece, ('replica', 'shard'), axis=0, tiled=True)]
    psum x1, blocking collectives: 6.93 us -> 56.6 us  [body(): norm_summed = lax.psum(trained_norm[0].astype(jnp.float32), 'replica')]
    all_gather x1, waiting for transfers between devices: 25 us -> 8.55 us  [body(): lax.all_gather(stored_rows.astype(jnp.bfloat16), 'replica', axis=0, tiled...]
    all_to_all x0 -> x1, starting transfers between devices: none -> 9.67 us  [body(): lax.all_to_all(jnp.stack([down_piece for _ in range(lax.axis_size(('repli...]
    unnamed x30 -> x28, local copies, waits for them, and re-layouts: 10 us -> 11.5 us
    unnamed x7 -> x6, waiting for transfers between devices: 38.1 us -> 38 us
  transfers between devices with their start and end apart: 6 -> 6, of which waited for: 6 -> 5; matrix products, arithmetic and copies ran while one was open for 4% -> 5% of each run, Pallas kernels for 0% -> 0%
where the time goes in v1:
time: 315 us
  waiting for transfers between devices  191 us (61%)
  blocking collectives  72.7 us (23%)
  local copies, waits for them, and re-layouts  17.5 us (6%)
  between operations  13.9 us (4%)
  starting transfers between devices  9.87 us (3%)
  other arithmetic  5.08 us (2%)
  matrix products  4.38 us (1%)
    all_gather x1, waiting for transfers between devices, body(): lax.all_gather(up_piece, ('replica', 'shard'), axis=0, tiled=True)  107 us
    psum x1, blocking collectives, body(): norm_summed = lax.psum(trained_norm[0].astype(jnp.float32), 'replica')  56.6 us
    unnamed x6, waiting for transfers between devices  38 us
    reduce_scatter x1, waiting for transfers between devices, body(): lax.psum_scatter(embed_terms.astype(jnp.bfloat16), 'replica', scatter_dim...  32.1 us
    unnamed x28, local copies, waits for them, and re-layouts  11.5 us
    all_to_all x1, starting transfers between devices, body(): lax.all_to_all(jnp.stack([down_piece for _ in range(lax.axis_size(('repli...  9.67 us
    all_to_all x1, blocking collectives, body(): lax.all_to_all(up_summed, 'tensor', split_axis=1, concat_axis=3, tiled=True)  8.59 us
    all_gather x1, waiting for transfers between devices, body(): lax.all_gather(stored_rows.astype(jnp.bfloat16), 'replica', axis=0, tiled...  8.55 us
  transfers between devices with their start and end apart: 6, of which 5 were waited for; matrix products, arithmetic and copies ran while one was open for 5% of the time, Pallas kernels for 0%

profile of v1, /device:TPU:1, one launch (start us, length us, event | category | flops | bytes accessed | tf_op | source)
XLA Modules:
  0.0 314.8 jit_solution(9496992198973500709)
XLA Ops:
  7.2 0.0 copy-start
  7.2 0.0 copy-start.1
  7.2 0.0 copy-start.3
  7.2 0.0 reduce-scatter.6.cloned.1.call-start
  7.3 0.0 copy-start.11
  7.3 0.7 reduce-scatter.6.cloned.1.call-update
  7.9 0.0 copy-start.6
  8.0 0.0 copy-start.7
  8.0 0.0 all-reduce.3.cloned.1.call-start
  8.0 1.7 copy_bitcast_fusion
  9.7 0.0 copy-start.4
  9.7 0.0 copy-start.5
  9.7 0.0 all-reduce.3.cloned.1.call-update
  9.7 0.0 reduce-scatter.4.cloned.1.call-start
  9.8 1.7 dynamic-slice_bitcast_fusion
  11.5 0.0 reduce-scatter.4.cloned.1.call-update
  11.5 0.0 all-gather.5.cloned.1.call-start
  11.6 32.1 %reduce-scatter.6.cloned.1.call-done = bf16[1,256,1024]{2,1,0:T(8,128)(2,1)} async-done(((bf16[4,256,1024]{2,1,0:T(8,128)(2,1)}), bf16[1,256,1024]{2,1,0:T(8,128)(2,1)}) %reduce-scatter.6.cloned.1.call-update) | async-done | bytes 524304 | tf_op jit(solution)/shard_map/reduce_scatter | solution.py:64
  43.6 0.0 copy-done
  43.6 0.0 copy-done.1
  43.6 2.2 fusion.1
  45.8 0.0 copy-done.3
  45.8 2.2 fusion.15
  48.0 0.0 all-gather.5.cloned.1.call-update
  48.1 0.0 all-gather.3.cloned.1.call-start
  48.1 0.0 copy-done.11
  48.1 0.6 dynamic-slice
  48.7 37.3 %all-reduce.3.cloned.1.call-done = bf16[4,2,8,2048]{3,2,0,1:T(8,128)(2,1)} async-done(((bf16[4,2,8,2048]{3,2,0,1:T(8,128)(2,1)}), bf16[4,2,8,2048]{3,2,0,1:T(8,128)(2,1)}) %all-reduce.3.cloned.1.call-update) | async-done | bytes 262160
  86.0 1.5 dynamic-slice_convert_fusion
  87.5 8.6 %all_to_all.33 = f32[1,2,8,2048]{3,2,0,1:T(8,128)S(1)} all-to-all(f32[1,2,8,2048]{3,2,0,1:T(8,128)S(1)} %dynamic-slice_convert_fusion), channel_id=1, replica_groups=mesh['replica'=4,'shard'=16,'tensor'=2] {'tensor'}, dimensions={1} | all-to-all | bytes 262144 | tf_op jit(solution)/shard_map/all_to_all | solution.py:54
  96.1 0.0 copy-done.6
  96.1 0.0 copy-done.7
  96.1 0.7 fusion.14
  96.9 7.5 %all_to_all.34 = bf16[8,2,2048]{2,0,1:T(8,128)(2,1)} all-to-all(bf16[8,2,2048]{2,0,1:T(8,128)(2,1)S(1)} %bitcast.54), channel_id=1, replica_groups=mesh['replica'=4,'shard'=16,'tensor'=2] {'tensor'}, dimensions={1} | all-to-all | bytes 131072 | tf_op jit(solution)/shard_map/all_to_all | solution.py:74
  104.4 0.0 all-gather.3.cloned.1.call-update
  104.4 5.9 %reduce-scatter.4.cloned.1.call-done = bf16[1,32,1024]{2,1,0:T(8,128)(2,1)} async-done(((bf16[4,32,1024]{2,1,0:T(8,128)(2,1)}), bf16[1,32,1024]{2,1,0:T(8,128)(2,1)}) %reduce-scatter.4.cloned.1.call-update) | async-done | bytes 65552 | tf_op jit(solution)/shard_map/reduce_scatter | solution.py:47
  110.3 0.0 copy-done.4
  110.3 0.0 copy-done.5
  110.3 1.6 convert_bitcast_fusion
  111.9 2.5 stack.5
  114.4 0.0 copy-start.10
  114.4 0.0 copy-start.8
  114.4 0.0 copy-start.9
  114.4 9.7 %all-to-all-start.2 = ((bf16[64,32,1024]{2,1,0:T(8,128)(2,1)}), bf16[64,32,1024]{2,1,0:T(8,128)(2,1)}, u32[]{:S(2)}, u32[]{:S(2)}) async-start(bf16[64,32,1024]{2,1,0:T(8,128)(2,1)} %stack.5), calls=%async_computation.3 | async-start | bytes 8388608 | tf_op jit(solution)/shard_map/all_to_all | solution.py:81
  124.1 0.0 copy-done.10
  124.1 56.6 %psum.7 = f32[2,1024]{1,0:T(2,128)S(1)} all-reduce(f32[2,1024]{1,0:T(2,128)S(1)} %bitcast_convert_fusion), channel_id=1, replica_groups=mesh['replica'=4,'shard'=16,'tensor'=2] {'replica'}, use_global_device_ids=true, to_apply=%region_3.4 | all-reduce | flops 2048 | bytes 16384 | tf_op jit(solution)/shard_map/psum | solution.py:59
  180.7 0.0 copy-done.8
  180.7 0.0 copy-done.9
  180.7 0.6 fusion.13
  181.4 0.6 fusion.8
  182.0 0.0 all-to-all-done.2
  182.0 8.6 %all-gather.5.cloned.1.call-done = bf16[1024,1024]{1,0:T(8,128)(2,1)} async-done(((bf16[256,1024]{1,0:T(8,128)(2,1)}), bf16[1024,1024]{1,0:T(8,128)(2,1)}) %all-gather.5.cloned.1.call-update) | async-done | bytes 2097168 | tf_op jit(solution)/shard_map/all_gather | solution.py:90
  190.6 106.8 %all-gather.3.cloned.1.call-done = bf16[1024,2048]{1,0:T(8,128)(2,1)} async-done(((bf16[16,2048]{1,0:T(8,128)(2,1)}), bf16[1024,2048]{1,0:T(8,128)(2,1)}) %all-gather.3.cloned.1.call-update) | async-done | bytes 4194320 | tf_op jit(solution)/shard_map/all_gather | solution.py:79
  297.4 4.8 %copy.39 = bf16[1024,2048]{1,0:T(8,128)(2,1)} copy(bf16[1024,2048]{1,0:T(8,128)(2,1)} %all-gather.3.cloned.1.call-done) | data formatting | bytes 8388608
  302.2 0.0 copy-start.2
  302.2 4.8 %copy.40 = bf16[2048,1024]{1,0:T(8,128)(2,1)} copy(bf16[2048,1024]{1,0:T(8,128)(2,1)} %bitcast.11) | data formatting | bytes 8388608
  307.0 0.0 copy-done.2
  307.0 1.3 copy.41
  (2 shorter events, 0.0 us)
Async XLA Ops:
  7.2 36.5 %copy-start = (f32[1024,64]{0,1:T(8,128)S(1)}, f32[1024,64]{0,1:T(8,128)}, u32[]{:S(2)}) copy-start(f32[1024,64]{0,1:T(8,128)} %param.25) | copy-start | bytes 786436
  7.2 36.5 %copy-start.1 = (f32[1,256,1024]{2,1,0:T(8,128)S(1)}, f32[1,256,1024]{2,1,0:T(8,128)}, u32[]{:S(2)}) copy-start(f32[1,256,1024]{2,1,0:T(8,128)} %param.21) | copy-start | bytes 3145732
  7.2 38.6 %copy-start.3 = (f32[1,256,64]{1,2,0:T(8,128)S(1)}, f32[1,256,64]{1,2,0:T(8,128)}, u32[]{:S(2)}) copy-start(f32[1,256,64]{1,2,0:T(8,128)} %param.22) | copy-start | bytes 196612
  7.2 36.4 %reduce-scatter.6.cloned.1.call-start = ((), (), s32[]{:S(2)}) async-start(), calls=%async_computation.7 | async-start | bytes 2621440 | tf_op jit(solution)/shard_map/reduce_scatter | solution.py:64
  7.3 40.9 %copy-start.11 = (u32[128]{0:T(128)S(1)}, u32[128]{0:T(128)}, u32[]{:S(2)}) copy-start(u32[128]{0:T(128)} %constant.47) | copy-start | bytes 1540
  7.9 88.2 %copy-start.6 = (f32[8,4096]{1,0:T(8,128)S(1)}, f32[8,4096]{1,0:T(8,128)}, u32[]{:S(2)}) copy-start(f32[8,4096]{1,0:T(8,128)} %param.17) | copy-start | bytes 393220
  8.0 88.2 %copy-start.7 = (f32[8,4096]{1,0:T(8,128)S(1)}, f32[8,4096]{1,0:T(8,128)}, u32[]{:S(2)}) copy-start(f32[8,4096]{1,0:T(8,128)} %param.18) | copy-start | bytes 393220
  8.0 78.0 %all-reduce.3.cloned.1.call-start = ((), (), s32[]{:S(2)}) async-start(), calls=%async_computation.9 | async-start | bytes 524288
  9.7 100.6 %copy-start.4 = (f32[1,32,1024]{2,1,0:T(8,128)S(1)}, f32[1,32,1024]{2,1,0:T(8,128)}, u32[]{:S(2)}) copy-start(f32[1,32,1024]{2,1,0:T(8,128)} %param.19) | copy-start | bytes 393220
  9.7 100.6 %copy-start.5 = (f32[1,32,1024]{2,1,0:T(8,128)S(1)}, f32[1,32,1024]{2,1,0:T(8,128)}, u32[]{:S(2)}) copy-start(f32[1,32,1024]{2,1,0:T(8,128)} %param.20) | copy-start | bytes 393220
  9.7 100.6 %reduce-scatter.4.cloned.1.call-start = ((), (), s32[]{:S(2)}) async-start(), calls=%async_computation.6 | async-start | bytes 327680 | tf_op jit(solution)/shard_map/reduce_scatter | solution.py:47
  11.5 179.0 %all-gather.5.cloned.1.call-start = ((), (), s32[]{:S(2)}) async-start(), calls=%async_computation.8 | async-start | bytes 2621440 | tf_op jit(solution)/shard_map/all_gather | solution.py:90
  48.1 249.3 %all-gather.3.cloned.1.call-start = ((), (), s32[]{:S(2)}) async-start(), calls=%async_computation.5 | async-start | bytes 4259840 | tf_op jit(solution)/shard_map/all_gather | solution.py:79
  114.4 9.7 %copy-start.10 = (bf16[1,2,1024]{2,1,0:T(2,128)(2,1)S(1)}, bf16[1,2,1024]{2,1,0:T(2,128)(2,1)}, u32[]{:S(2)}) copy-start(bf16[1,2,1024]{2,1,0:T(2,128)(2,1)} %param.16) | copy-start | bytes 12292
  114.4 66.3 %copy-start.8 = (f32[2,1024]{1,0:T(2,128)S(1)}, f32[2,1024]{1,0:T(2,128)}, u32[]{:S(2)}) copy-start(f32[2,1024]{1,0:T(2,128)} %param.23) | copy-start | bytes 24580
  114.4 66.3 %copy-start.9 = (f32[2,1024]{1,0:T(2,128)S(1)}, f32[2,1024]{1,0:T(2,128)}, u32[]{:S(2)}) copy-start(f32[2,1024]{1,0:T(2,128)} %param.24) | copy-start | bytes 24580
  114.4 67.6 %all-to-all-start.2 = ((bf16[64,32,1024]{2,1,0:T(8,128)(2,1)}), bf16[64,32,1024]{2,1,0:T(8,128)(2,1)}, u32[]{:S(2)}, u32[]{:S(2)}) async-start(bf16[64,32,1024]{2,1,0:T(8,128)(2,1)} %stack.5), calls=%async_computation.3 | async-start | bytes 8388608 | tf_op jit(solution)/shard_map/all_to_all | solution.py:81
  302.2 4.8 %copy-start.2 = (bf16[1024,1024]{1,0:T(8,128)(2,1)S(1)}, bf16[1024,1024]{1,0:T(8,128)(2,1)}, u32[]{:S(2)}) copy-start(bf16[1024,1024]{1,0:T(8,128)(2,1)} %all-gather.5.cloned.1.call-done) | copy-start | bytes 6291460
Sparse Core Ops, SparseCore 0:
  10.4 33.1 reduce-scatter.5
  46.7 39.3 all-reduce.2
  89.0 21.2 reduce-scatter.3
  112.5 78.0 all-gather.4
  192.2 105.1 all-gather.2
